TPU v7x, 128 devices: a whole 4x4x4 slice. The times are simulated.
128 devices in a mesh: rows: 16 (over x, z), cols: 8 (over y, core).
Axes of the slice: x: 4, y: 4, z: 4, core: 2. Of those that a mesh axis runs over, the one named last changes fastest.
Arguments:
- counts: int32 [2048, 512, 512], P(('rows', 'cols')), may hold values from 0 to 1024, as said below
- shard_rows: int32 [2048], P(('rows', 'cols')), may hold values from 0 to 255, as said below
- shard_cols: int32 [2048], P(('rows', 'cols')), may hold values from 0 to 255, as said below
- listed: int32 [128], P(('rows', 'cols')), may hold values from 2 to 16, as said below
- row_embed: float32 [131072, 256], P(('rows', 'cols')), may hold values from -1.5 to 1.5
- row_accum: float32 [131072, 256], P(('rows', 'cols')), may hold values from 300 to 10000
- row_offset: bfloat16 [131072], P(('rows', 'cols')), may hold values from -3 to -1
- col_embed: float32 [131072, 256], P(('rows', 'cols')), may hold values from -1.5 to 1.5
- col_accum: float32 [131072, 256], P(('rows', 'cols')), may hold values from 300 to 10000
- col_offset: bfloat16 [131072], P(('rows', 'cols')), may hold values from -3 to -1
Outputs:
- row_trained: float32 [131072, 256], P(('rows', 'cols'))
- col_trained: float32 [131072, 256], P(('rows', 'cols'))
Inputs may be any that keep to these rules, and one draw needn't show every extreme that they name: `shard_rows`: entry q belongs to holder h = q // 16, the device at rows index h // 8 and cols index h % 8. Row block g is owned by device g // 2 in the same order. The row block of a listed entry is owned by a device with its holder's cols index; the listed entries of one holder use at most 1 different row blocks of any one owner, and in some holder exactly 1 of each of the 16 owners with its cols index. `shard_cols`: column block c is owned by device c // 2. The column block of a listed entry is owned by a device with its holder's rows index. No holder lists the same pair of blocks twice. The listed entries of holder h are its first listed[h] ones; its other entries and their counts take no part. `counts`: zero where the pair of items never occurs together.
All inputs are finite; a program needn't handle non-finite values.
Results may differ from a plain program's by a relative error of at most 0.0014.
Values may be sent and summed in bfloat16 or wider, within the bound.
A program may use at most 192 MiB of HBM per device.

v0:
```python
import jax
import jax.numpy as jnp
from jax import lax
from jax.sharding import PartitionSpec as P

learning_rate = 0.5
conf_base = 0.1
conf_scale = 0.25
shard_group = 4


def slopes(cell_counts, scores, row_shift, col_shift):
    floored = jnp.maximum(cell_counts, 1).astype(jnp.float32)
    pointwise = jnp.log(floored) + row_shift[:, :, None] + col_shift[:, None, :]
    weight = conf_base + conf_scale * jnp.sqrt(floored)
    return jnp.where(
        cell_counts > 0, weight * (scores - pointwise), jax.nn.sigmoid(scores - pointwise)
    )


def process(
    count_tiles, live_count, row_pool, row_shifts, row_index, col_pool, col_shifts, col_index
):
    turns = count_tiles.shape[0] // shard_group

    def one_turn(turn_index, totals):
        row_grad, col_grad = totals
        first = turn_index * shard_group
        tile_group = lax.dynamic_slice_in_dim(count_tiles, first, shard_group, 0)
        row_slots = lax.dynamic_slice_in_dim(row_index, first, shard_group, 0)
        col_slots = lax.dynamic_slice_in_dim(col_index, first, shard_group, 0)
        row_vectors = jnp.take(row_pool, row_slots, axis=0)
        col_vectors = jnp.take(col_pool, col_slots, axis=0)
        scores = jnp.einsum(
            "sbd,sed->sbe", row_vectors, col_vectors, preferred_element_type=jnp.float32
        )
        row_shift = jnp.take(row_shifts, row_slots, axis=0).astype(jnp.float32)
        col_shift = jnp.take(col_shifts, col_slots, axis=0).astype(jnp.float32)
        slope_full = slopes(tile_group, scores, row_shift, col_shift)
        in_list = first + jnp.arange(shard_group, dtype=jnp.int32) < live_count
        slope_full = jnp.where(in_list[:, None, None], slope_full, jnp.zeros_like(slope_full))
        slope_half = slope_full.astype(jnp.bfloat16)
        row_terms = jnp.einsum(
            "sbe,sed->sbd", slope_half, col_vectors, preferred_element_type=jnp.float32
        )
        col_terms = jnp.einsum(
            "sbe,sbd->sed", slope_half, row_vectors, preferred_element_type=jnp.float32
        )
        return (row_grad.at[row_slots].add(row_terms), col_grad.at[col_slots].add(col_terms))

    start = (jnp.zeros(row_pool.shape, jnp.float32), jnp.zeros(col_pool.shape, jnp.float32))
    return lax.fori_loop(0, turns, one_turn, start)


def on_device(
    counts,
    shard_rows,
    shard_cols,
    listed,
    row_embed,
    row_accum,
    row_offset,
    col_embed,
    col_accum,
    col_offset,
):
    block_items = counts.shape[1]
    features = row_embed.shape[1]
    row_owned = row_embed.shape[0] // block_items
    col_owned = col_embed.shape[0] // block_items
    col_devices = lax.axis_size("cols")
    live_count = listed[0]
    row_set = shard_rows // row_owned // col_devices * row_owned + shard_rows % row_owned
    col_set = shard_cols // col_owned % col_devices * col_owned + shard_cols % col_owned
    row_half = row_embed.astype(jnp.bfloat16)
    col_half = col_embed.astype(jnp.bfloat16)
    col_pool = lax.all_gather(col_half, "cols", axis=0, tiled=True)
    col_shifts = lax.all_gather(col_offset, "cols", axis=0, tiled=True)
    row_pool = lax.all_gather(row_half, "rows", axis=0, tiled=True)
    row_shifts = lax.all_gather(row_offset, "rows", axis=0, tiled=True)
    row_pool = row_pool.reshape(-1, block_items, features)
    row_shifts = row_shifts.reshape(-1, block_items)
    row_part, col_part = process(
        counts,
        live_count,
        row_pool,
        row_shifts,
        row_set,
        col_pool.reshape(-1, block_items, features),
        col_shifts.reshape(-1, block_items),
        col_set,
    )
    row_grad = lax.psum_scatter(
        row_part.reshape(-1, features), "rows", scatter_dimension=0, tiled=True
    )
    col_grad = lax.psum_scatter(
        col_part.reshape(-1, features), "cols", scatter_dimension=0, tiled=True
    )
    row_accum = row_accum + row_grad * row_grad
    col_accum = col_accum + col_grad * col_grad
    row_embed = row_embed - learning_rate * row_grad / jnp.sqrt(row_accum)
    col_embed = col_embed - learning_rate * col_grad / jnp.sqrt(col_accum)
    return (row_embed, col_embed)


def solution(mesh):
    in_specs = (
        P(("rows", "cols"), None, None),
        P(("rows", "cols")),
        P(("rows", "cols")),
        P(("rows", "cols")),
        P(("rows", "cols"), None),
        P(("rows", "cols"), None),
        P(("rows", "cols")),
        P(("rows", "cols"), None),
        P(("rows", "cols"), None),
        P(("rows", "cols")),
    )
    out_specs = (P(("rows", "cols"), None), P(("rows", "cols"), None))
    return jax.shard_map(
        on_device, mesh=mesh, in_specs=in_specs, out_specs=out_specs, check_vma=False
    )
```

profile of v0, /device:TPU:1, one launch (start us, length us, event | category | flops | bytes accessed | tf_op | source)
XLA Modules:
  0.0 412.6 jit_solution(9346505922726020721)
XLA Ops:
  11.6 13.5 %all_gather.15 = bf16[8192]{0:T(1024)(128)(2,1)S(1)} all-gather(bf16[1024]{0:T(1024)(128)(2,1)S(1)} %copy-done.3), channel_id=1, replica_groups=mesh['rows'=16,'cols'=8] {'cols'}, dimensions={0}, use_global_device_ids=true | all-gather | bytes 18432 | tf_op jit(solution)/shard_map/all_gather | solution.py:78
  25.1 21.2 %all_gather.14 = bf16[16384]{0:T(1024)(128)(2,1)S(1)} all-gather(bf16[1024]{0:T(1024)(128)(2,1)S(1)} %copy-done.4), channel_id=1, replica_groups=mesh['rows'=16,'cols'=8] {'rows'}, dimensions={0}, use_global_device_ids=true | all-gather | bytes 34816 | tf_op jit(solution)/shard_map/all_gather | solution.py:80
  46.4 72.6 %all-gather.3.cloned.1.call-done = bf16[16384,256]{1,0:T(8,128)(2,1)} async-done(((bf16[1024,256]{1,0:T(8,128)(2,1)}), bf16[16384,256]{1,0:T(8,128)(2,1)}) %all-gather.3.cloned.1.call-update) | async-done | bytes 8388624 | tf_op jit(solution)/shard_map/all_gather | solution.py:79
  119.0 4.1 broadcast_in_dim.102
  123.2 7.7 %broadcast_in_dim.101 = f32[32,512,256]{2,1,0:T(8,128)} broadcast(f32[]{:T(128)} %constant.184.clone.1), dimensions={} | broadcast | bytes 16777220 | tf_op jit(solution)/shard_map/broadcast_in_dim | solution.py:51
  130.9 106.7 %while.15 = (s32[]{:T(128)}, f32[32,512,256]{2,1,0:T(8,128)}, f32[16,512,256]{2,1,0:T(8,128)}, s32[16]{0:T(128)S(1)}, s32[]{:T(128)}, /*index=5*/s32[16,512,512]...) while((s32[]{:T(128)}, f32[32,512,256]{2,1,0:T(8,128)}, ...), condition=%wide.region_3.4_spmd, body=%wide.region_0.3_spmd.sunk | while | flops 1629497344 | bytes 35717552 | solution.py:52
  132.9 4.0 gather_fusion.2
  139.7 5.6 %select_convert_fusion.8 = bf16[4,512,512]{2,1,0:T(8,128)(2,1)S(1)} fusion(s32[16,512,512]{2,1,0:T(8,128)} %get-tuple-element.329, s32[]{:T(128)S(6)} %select_n.171, f32[4,512]{1,0:T(4,128)S(1)} %select_convert_fusion.6, f32[4,512]{1,0:T(4,128)S(1)} %select_convert_fusion.7, pred[4]{0:T(512)(128)(4,1)S(1)} %add_compare_fusion.2, ...), kind=kOutput, calls=%fused_computation.6.clone.1 | convolution fusion | flops 553648128 | bytes 8405008 | tf_op jit(solution)/shard_map/while/body/eval_jaxpr/sbd,sed->sbe/dot_general | solution.py:34
  148.3 4.8 %scatter_fusion.1 = f32[16,512,256]{2,1,0:T(8,128)} fusion(f32[16,512,256]{2,1,0:T(8,128)} %get-tuple-element.311, s32[4]{0:T(128)S(1)} %get-tuple-element.291, f32[4,512,256]{2,1,0:T(8,128)} %fusion.18), kind=kCustom, calls=%fused_computation.5.clone.1 | custom fusion | flops 524288 | bytes 6291472 | tf_op jit(solution)/shard_map/while/body/eval_jaxpr/scatter-add | solution.py:49
  153.1 4.3 %scatter_fusion = f32[32,512,256]{2,1,0:T(8,128)} fusion(f32[32,512,256]{2,1,0:T(8,128)} %get-tuple-element.310, s32[4]{0:T(128)S(1)} %get-tuple-element.290, f32[4,512,256]{2,1,0:T(8,128)S(1)} %fusion.17), kind=kCustom, calls=%fused_computation.4.clone.1 | custom fusion | flops 524288 | bytes 6291472 | tf_op jit(solution)/shard_map/while/body/eval_jaxpr/scatter-add | solution.py:49
  159.5 4.0 gather_fusion.2
  166.3 5.6 %select_convert_fusion.8 = bf16[4,512,512]{2,1,0:T(8,128)(2,1)S(1)} fusion(s32[16,512,512]{2,1,0:T(8,128)} %get-tuple-element.329, s32[]{:T(128)S(6)} %select_n.171, f32[4,512]{1,0:T(4,128)S(1)} %select_convert_fusion.6, f32[4,512]{1,0:T(4,128)S(1)} %select_convert_fusion.7, pred[4]{0:T(512)(128)(4,1)S(1)} %add_compare_fusion.2, ...), kind=kOutput, calls=%fused_computation.6.clone.1 | convolution fusion | flops 553648128 | bytes 8405008 | tf_op jit(solution)/shard_map/while/body/eval_jaxpr/sbd,sed->sbe/dot_general | solution.py:34
  174.9 4.9 %scatter_fusion.1 = f32[16,512,256]{2,1,0:T(8,128)} fusion(f32[16,512,256]{2,1,0:T(8,128)} %get-tuple-element.311, s32[4]{0:T(128)S(1)} %get-tuple-element.291, f32[4,512,256]{2,1,0:T(8,128)} %fusion.18), kind=kCustom, calls=%fused_computation.5.clone.1 | custom fusion | flops 524288 | bytes 6291472 | tf_op jit(solution)/shard_map/while/body/eval_jaxpr/scatter-add | solution.py:49
  179.8 4.3 %scatter_fusion = f32[32,512,256]{2,1,0:T(8,128)} fusion(f32[32,512,256]{2,1,0:T(8,128)} %get-tuple-element.310, s32[4]{0:T(128)S(1)} %get-tuple-element.290, f32[4,512,256]{2,1,0:T(8,128)S(1)} %fusion.17), kind=kCustom, calls=%fused_computation.4.clone.1 | custom fusion | flops 524288 | bytes 6291472 | tf_op jit(solution)/shard_map/while/body/eval_jaxpr/scatter-add | solution.py:49
  186.1 4.0 gather_fusion.2
  193.0 5.6 %select_convert_fusion.8 = bf16[4,512,512]{2,1,0:T(8,128)(2,1)S(1)} fusion(s32[16,512,512]{2,1,0:T(8,128)} %get-tuple-element.329, s32[]{:T(128)S(6)} %select_n.171, f32[4,512]{1,0:T(4,128)S(1)} %select_convert_fusion.6, f32[4,512]{1,0:T(4,128)S(1)} %select_convert_fusion.7, pred[4]{0:T(512)(128)(4,1)S(1)} %add_compare_fusion.2, ...), kind=kOutput, calls=%fused_computation.6.clone.1 | convolution fusion | flops 553648128 | bytes 8405008 | tf_op jit(solution)/shard_map/while/body/eval_jaxpr/sbd,sed->sbe/dot_general | solution.py:34
  201.5 5.1 %scatter_fusion.1 = f32[16,512,256]{2,1,0:T(8,128)} fusion(f32[16,512,256]{2,1,0:T(8,128)} %get-tuple-element.311, s32[4]{0:T(128)S(1)} %get-tuple-element.291, f32[4,512,256]{2,1,0:T(8,128)} %fusion.18), kind=kCustom, calls=%fused_computation.5.clone.1 | custom fusion | flops 524288 | bytes 6291472 | tf_op jit(solution)/shard_map/while/body/eval_jaxpr/scatter-add | solution.py:49
  206.6 4.2 %scatter_fusion = f32[32,512,256]{2,1,0:T(8,128)} fusion(f32[32,512,256]{2,1,0:T(8,128)} %get-tuple-element.310, s32[4]{0:T(128)S(1)} %get-tuple-element.290, f32[4,512,256]{2,1,0:T(8,128)S(1)} %fusion.17), kind=kCustom, calls=%fused_computation.4.clone.1 | custom fusion | flops 524288 | bytes 6291472 | tf_op jit(solution)/shard_map/while/body/eval_jaxpr/scatter-add | solution.py:49
  212.9 4.0 gather_fusion.2
  219.7 5.6 %select_convert_fusion.8 = bf16[4,512,512]{2,1,0:T(8,128)(2,1)S(1)} fusion(s32[16,512,512]{2,1,0:T(8,128)} %get-tuple-element.329, s32[]{:T(128)S(6)} %select_n.171, f32[4,512]{1,0:T(4,128)S(1)} %select_convert_fusion.6, f32[4,512]{1,0:T(4,128)S(1)} %select_convert_fusion.7, pred[4]{0:T(512)(128)(4,1)S(1)} %add_compare_fusion.2, ...), kind=kOutput, calls=%fused_computation.6.clone.1 | convolution fusion | flops 553648128 | bytes 8405008 | tf_op jit(solution)/shard_map/while/body/eval_jaxpr/sbd,sed->sbe/dot_general | solution.py:34
  228.3 5.0 %scatter_fusion.1 = f32[16,512,256]{2,1,0:T(8,128)} fusion(f32[16,512,256]{2,1,0:T(8,128)} %get-tuple-element.311, s32[4]{0:T(128)S(1)} %get-tuple-element.291, f32[4,512,256]{2,1,0:T(8,128)} %fusion.18), kind=kCustom, calls=%fused_computation.5.clone.1 | custom fusion | flops 524288 | bytes 6291472 | tf_op jit(solution)/shard_map/while/body/eval_jaxpr/scatter-add | solution.py:49
  233.3 4.3 %scatter_fusion = f32[32,512,256]{2,1,0:T(8,128)} fusion(f32[32,512,256]{2,1,0:T(8,128)} %get-tuple-element.310, s32[4]{0:T(128)S(1)} %get-tuple-element.290, f32[4,512,256]{2,1,0:T(8,128)S(1)} %fusion.17), kind=kCustom, calls=%fused_computation.4.clone.1 | custom fusion | flops 524288 | bytes 6291472 | tf_op jit(solution)/shard_map/while/body/eval_jaxpr/scatter-add | solution.py:49
  238.2 51.0 %reduce-scatter.5.cloned.1.call-done = f32[1024,256]{1,0:T(8,128)} async-done(((f32[8192,256]{1,0:T(8,128)}), f32[1024,256]{1,0:T(8,128)}) %reduce-scatter.5.cloned.1.call-update) | async-done | bytes 1048592 | tf_op jit(solution)/shard_map/reduce_scatter | solution.py:96
  291.7 111.7 %reduce-scatter.3.cloned.1.call-done = f32[1024,256]{1,0:T(8,128)} async-done(((f32[16384,256]{1,0:T(8,128)}), f32[1024,256]{1,0:T(8,128)}) %reduce-scatter.3.cloned.1.call-update) | async-done | bytes 1048592 | tf_op jit(solution)/shard_map/reduce_scatter | solution.py:93
  (74 shorter events, 41.5 us)
Async XLA Ops:
  7.2 4.4 %copy-start.3 = (bf16[1024]{0:T(1024)(128)(2,1)S(1)}, bf16[1024]{0:T(1024)(128)(2,1)}, u32[]{:S(2)}) copy-start(bf16[1024]{0:T(1024)(128)(2,1)} %param.21) | copy-start | bytes 6148
  7.2 17.9 %copy-start.4 = (bf16[1024]{0:T(1024)(128)(2,1)S(1)}, bf16[1024]{0:T(1024)(128)(2,1)}, u32[]{:S(2)}) copy-start(bf16[1024]{0:T(1024)(128)(2,1)} %param.18) | copy-start | bytes 6148
  7.2 39.2 %copy-start.6 = (s32[16]{0:T(128)S(1)}, s32[16]{0:T(128)}, u32[]{:S(2)}) copy-start(s32[16]{0:T(128)} %param.14) | copy-start | bytes 196
  7.2 39.2 %copy-start.5 = (s32[16]{0:T(128)S(1)}, s32[16]{0:T(128)}, u32[]{:S(2)}) copy-start(s32[16]{0:T(128)} %param.13) | copy-start | bytes 196
  7.2 39.2 %all-gather.5.cloned.1.call-start = ((), (), s32[]{:S(2)}) async-start(), calls=%async_computation.3 | async-start | bytes 4718592 | tf_op jit(solution)/shard_map/all_gather | solution.py:77
  9.3 109.7 %all-gather.3.cloned.1.call-start = ((), (), s32[]{:S(2)}) async-start(), calls=%async_computation.2 | async-start | bytes 8912896 | tf_op jit(solution)/shard_map/all_gather | solution.py:79
  11.5 277.8 %reduce-scatter.5.cloned.1.call-start = ((), (), s32[]{:S(2)}) async-start(), calls=%async_computation.5 | async-start | bytes 9437184 | tf_op jit(solution)/shard_map/reduce_scatter | solution.py:96
  237.6 165.7 %reduce-scatter.3.cloned.1.call-start = ((), (), s32[]{:S(2)}) async-start(), calls=%async_computation.4 | async-start | bytes 17825792 | tf_op jit(solution)/shard_map/reduce_scatter | solution.py:93
  237.7 51.6 %copy-start = (f32[1024,256]{1,0:T(8,128)S(1)}, f32[1024,256]{1,0:T(8,128)}, u32[]{:S(2)}) copy-start(f32[1024,256]{1,0:T(8,128)} %param.19) | copy-start | bytes 3145732
  237.7 51.6 %copy-start.2 = (f32[1024,256]{1,0:T(8,128)S(1)}, f32[1024,256]{1,0:T(8,128)}, u32[]{:S(2)}) copy-start(f32[1024,256]{1,0:T(8,128)} %param.20) | copy-start | bytes 3145732
  238.2 165.1 %copy-start.1 = (f32[1024,256]{1,0:T(8,128)S(1)}, f32[1024,256]{1,0:T(8,128)}, u32[]{:S(2)}) copy-start(f32[1024,256]{1,0:T(8,128)} %param.16) | copy-start | bytes 3145732
Sparse Core Ops, SparseCore 0:
  10.3 35.6 all-gather.4
  48.7 70.2 all-gather.2
  237.7 51.4 reduce-scatter.4
  292.5 110.7 reduce-scatter.2
where the time goes:
time: 413 us
  waiting for transfers between devices  236 us (57%)
  other arithmetic  49.8 us (12%)
  local copies, waits for them, and re-layouts  43.6 us (11%)
  blocking collectives  34.7 us (8%)
  matrix products  34.3 us (8%)
  between operations  13.9 us (3%)
    reduce_scatter x1, waiting for transfers between devices, on_device(): lax.psum_scatter(row_part.reshape(-1, features), 'rows', scatter_dimensio...  112 us
    all_gather x1, waiting for transfers between devices, on_device(): row_pool = lax.all_gather(row_half, 'rows', axis=0, tiled=True)  72.6 us
    reduce_scatter x1, waiting for transfers between devices, on_device(): lax.psum_scatter(col_part.reshape(-1, features), 'cols', scatter_dimensio...  51 us
    dot_general x4, matrix products, one_turn(): jnp.einsum('sbd,sed->sbe', row_vectors, col_vectors, preferred_element_ty...  22.2 us
    all_gather x1, blocking collectives, on_device(): row_shifts = lax.all_gather(row_offset, 'rows', axis=0, tiled=True)  21.2 us
    scatter-add x4, other arithmetic, one_turn(): col_grad.at[col_slots].add(col_terms)  19.8 us
    scatter-add x4, other arithmetic, one_turn(): row_grad.at[row_slots].add(row_terms)  17.1 us
    gather x4, local copies, waits for them, and re-layouts, one_turn(): row_vectors = jnp.take(row_pool, row_slots, axis=0)  16 us
  transfers between devices with their start and end apart: 4, of which 3 were waited for; matrix products, arithmetic and copies ran while one was open for 1% of the time, Pallas kernels for 0%

commit v1 on v0

v1 whole, which is shorter than its diff:
```python
import functools

import jax
import jax.numpy as jnp
from jax import lax
from jax.experimental import pallas as pl
from jax.experimental.pallas import tpu as pltpu
from jax.sharding import PartitionSpec as P

learning_rate = 0.5
conf_base = 0.1
conf_scale = 0.25
SIDE = 4
PAD = 16
FLOOR = 1.0 / 16.0
CODE = 32766.0 / 30.0
MESH = pl.DeviceIdType.MESH
ANY = pl.BlockSpec(memory_space=pl.ANY)


def encode(term):
    level = jnp.log2(1.0 + jnp.abs(term) * (1.0 / FLOOR)) * CODE + 0.5
    whole = level.astype(jnp.int32)
    return jnp.where(term < 0.0, -whole, whole).astype(jnp.int16)


def decode(code):
    level = code.astype(jnp.int32).astype(jnp.float32)
    size = jnp.exp2(jnp.abs(level) * (1.0 / CODE)) * FLOOR - FLOOR
    return jnp.where(level < 0.0, -size, size)


def place():
    row, col = lax.axis_index("rows"), lax.axis_index("cols")
    return row // SIDE, row % SIDE, col // 2, col % 2


def device(x, y, z, core):
    return (x * SIDE + z, y * 2 + core)


def turn(at, by):
    return lax.rem(at + (by + SIDE), SIDE)


class Copies:
    def __init__(self, send_sems, recv_sems):
        self.send_sems, self.recv_sems, self.started = send_sems, recv_sems, []

    def start(self, source, target, to):
        at = len(self.started)
        copy = pltpu.make_async_remote_copy(
            src_ref=source,
            dst_ref=target,
            send_sem=self.send_sems.at[at],
            recv_sem=self.recv_sems.at[at],
            device_id=to,
            device_id_type=MESH,
        )
        copy.start()
        self.started.append(copy)
        return copy

    def finish(self):
        for copy in self.started:
            copy.wait_send()


def greet(peers):
    barrier = pltpu.get_barrier_semaphore()
    for peer in peers:
        pl.semaphore_signal(barrier, inc=1, device_id=peer, device_id_type=MESH)
    pl.semaphore_wait(barrier, len(peers))


def gather_kernel(row_ref, col_ref, sel_ref, row_pool, col_pool, sel_in, send_sems, recv_sems, local_sems):
    x, z, y, core = place()
    row, col = lax.axis_index("rows"), lax.axis_index("cols")
    block_items = row_ref.shape[1] - PAD
    parts = (pl.ds(0, block_items // 2), pl.ds(block_items // 2, block_items // 2 + PAD))
    others = [(dx, dz) for dx in range(SIDE) for dz in range(SIDE) if (dx, dz) != (0, 0)]
    far = [device(turn(x, dx), y, turn(z, dz), core) for dx, dz in others]
    along_y = [device(x, turn(y, d), z, core) for d in (1, -1)]
    partner = device(x, y, z, 1 - core)
    greet(far + along_y + [partner])
    net = Copies(send_sems, recv_sems)

    own_row = pltpu.make_async_copy(row_ref, row_pool.at[row], local_sems.at[0])
    own_col = pltpu.make_async_copy(col_ref, col_pool.at[col], local_sems.at[1])

    def hop(axis, by):
        if axis == 0:
            return device(turn(x, by), y, z, core)
        return device(x, y, turn(z, by), core)

    def pool(block, first, second, part=None):
        dx, dz = (first, second) if block == 0 else (second, first)
        ref = row_pool.at[turn(x, dx) * SIDE + turn(z, dz), block]
        return ref if part is None else ref.at[parts[part]]

    def own(block, part=None):
        ref = row_ref.at[block]
        return ref if part is None else ref.at[parts[part]]

    axes = ((0, 1), (1, 0))
    one, two, relay_one, relay_two = {}, {}, {}, {}
    for block in (0, 1):
        for by in (1, -1):
            one[block, by] = net.start(own(block), pool(block, 0, 0), hop(axes[block][0], by))
    y_own = [net.start(col_ref, col_pool.at[col], to) for to in along_y]
    core_own = net.start(col_ref, col_pool.at[col], partner)
    for block in (0, 1):
        for by in (1, -1):
            two[block, 0, by] = net.start(own(block), pool(block, 0, 0), hop(axes[block][1], by))
    own_row.start()
    own_col.start()
    chosen = [
        net.start(sel_ref.at[turn(x, dx) * SIDE + turn(z, dz)], sel_in.at[row], to)
        for (dx, dz), to in zip(others, far)
    ]
    for by in (1, -1):
        for block in (0, 1):
            one[block, by].wait_recv()
            part = 0 if by == 1 else 1
            relay_one[block, by] = net.start(
                pool(block, -by, 0, part), pool(block, -by, 0, part), hop(axes[block][0], by)
            )
            for way in (1, -1):
                two[block, -by, way] = net.start(
                    pool(block, -by, 0), pool(block, -by, 0), hop(axes[block][1], way)
                )
    col_of = lambda d: turn(y, d) * 2 + core
    to_core, relay_y = [], []
    for at, by in enumerate((1, -1)):
        y_own[at].wait_recv()
        half = 0 if by == 1 else 1
        source = col_pool.at[col_of(-by), half]
        relay_y.append(net.start(source, source, along_y[at]))
        to_core.append(net.start(col_pool.at[col_of(-by)], col_pool.at[col_of(-by)], partner))

    def second_relays(first):
        for by in (1, -1):
            for block in (0, 1):
                two[block, first, by].wait_recv()
                part = 0 if by == 1 else 1
                relay_two[block, first, by] = net.start(
                    pool(block, first, -by, part), pool(block, first, -by, part), hop(axes[block][1], by)
                )

    second_relays(0)
    for block in (0, 1):
        for by in (1, -1):
            relay_one[block, by].wait_recv()
        for way in (1, -1):
            two[block, 2, way] = net.start(pool(block, 2, 0), pool(block, 2, 0), hop(axes[block][1], way))
    for copy in relay_y:
        copy.wait_recv()
    to_core.append(net.start(col_pool.at[col_of(2)], col_pool.at[col_of(2)], partner))
    for first in (-1, 1, 2):
        second_relays(first)
    for copy in relay_two.values():
        copy.wait_recv()
    for copy in [core_own] + to_core + chosen:
        copy.wait_recv()
    net.finish()
    own_row.wait()
    own_col.wait()


GATHER_COPIES = 40 + 2 + 1 + 2 + 3 + 15


def gather(row_packed, col_packed, chosen):
    blocks, tall, features = row_packed.shape
    owners, around = SIDE * SIDE, SIDE * 2
    return pl.pallas_call(
        gather_kernel,
        out_shape=(
            jax.ShapeDtypeStruct((owners,) + row_packed.shape, jnp.bfloat16),
            jax.ShapeDtypeStruct((around,) + col_packed.shape, jnp.bfloat16),
            jax.ShapeDtypeStruct(chosen.shape, jnp.int32),
        ),
        in_specs=[ANY] * 3,
        out_specs=(ANY,) * 3,
        scratch_shapes=[
            pltpu.SemaphoreType.DMA((GATHER_COPIES,)),
            pltpu.SemaphoreType.DMA((GATHER_COPIES,)),
            pltpu.SemaphoreType.DMA((2,)),
        ],
        compiler_params=pltpu.CompilerParams(collective_id=0, has_side_effects=True),
        name="gather_blocks",
    )(row_packed, col_packed, chosen)


LIVE, SLOT, OWNER, ROW, COL, ROW_FIRST, COL_FIRST, COL_USED = range(8)


def slots_kernel(plan, counts_ref, row_ref, col_ref, row_out, col_out, row_sum, col_sum, slope_ref):
    at = pl.program_id(0)
    block_items, features = row_sum.shape
    group = min(128, block_items)

    def offsets(ref):
        wide = ref[0, block_items:, :].astype(jnp.float32)
        pieces = [wide[i : i + 1] for i in range(block_items // features)]
        return pieces[0] if len(pieces) == 1 else jnp.concatenate(pieces, axis=1)

    @pl.when(at < plan[LIVE, 0])
    def _():
        col_vectors = col_ref[0, :block_items, :]
        row_shift = jnp.broadcast_to(offsets(row_ref), (8, block_items)).T[:, :1]
        col_shift = offsets(col_ref)
        for first in range(0, block_items, group):
            rows = slice(first, first + group)
            scores = lax.dot_general(
                row_ref[0, rows, :], col_vectors, (((1,), (1,)), ((), ())), preferred_element_type=jnp.float32
            )
            cells = counts_ref[0, rows, :].astype(jnp.float32)
            floored = jnp.maximum(cells, 1.0)
            gap = scores - row_shift[rows] - col_shift - jnp.log(floored)
            weight = conf_base + conf_scale * (floored * lax.rsqrt(floored))
            slope = jnp.where(cells > 0.0, weight * gap, 0.5 * jnp.tanh(0.5 * gap) + 0.5)
            slope_ref[rows, :] = slope.astype(jnp.bfloat16)
        slope = slope_ref[...]
        row_term = jnp.dot(slope, col_vectors, preferred_element_type=jnp.float32)

        @pl.when(plan[ROW_FIRST, at] == 1)
        def _():
            row_sum[...] = row_term

        @pl.when(plan[ROW_FIRST, at] == 0)
        def _():
            row_sum[...] += row_term

        @pl.when(plan[ROW_FIRST, at + 1] == 1)
        def _():
            row_out[0] = encode(row_sum[...])

        col_term = lax.dot_general(
            row_ref[0, :block_items, :], slope, (((0,), (0,)), ((), ())), preferred_element_type=jnp.float32
        )
        which = plan[COL, at]

        @pl.when(plan[COL_FIRST, at] == 1)
        def _():
            col_sum[which] = col_term

        @pl.when(plan[COL_FIRST, at] == 0)
        def _():
            col_sum[which] += col_term

    @pl.when(at == pl.num_programs(0) - 1)
    def _():
        def one(which, carry):
            @pl.when(plan[COL_USED, which] == 1)
            def _():
                col_out[which] = encode(col_sum[which])

            @pl.when(plan[COL_USED, which] == 0)
            def _():
                col_out[which] = jnp.zeros(col_out.shape[1:], jnp.int16)

            return carry

        lax.fori_loop(0, col_out.shape[0], one, 0)


def slots(plan, counts, row_pool, col_pool):
    count, block_items, unused = counts.shape
    owners, row_blocks, tall, features = row_pool.shape
    row_pool = row_pool.reshape(-1, tall, features)
    col_pool = col_pool.reshape(-1, tall, features)
    col_blocks = col_pool.shape[0]
    grid_spec = pltpu.PrefetchScalarGridSpec(
        num_scalar_prefetch=1,
        grid=(count,),
        in_specs=[
            pl.BlockSpec((1, block_items, block_items), lambda i, plan: (plan[SLOT, i], 0, 0)),
            pl.BlockSpec((1, tall, features), lambda i, plan: (plan[ROW, i], 0, 0)),
            pl.BlockSpec((1, tall, features), lambda i, plan: (plan[COL, i], 0, 0)),
        ],
        out_specs=(
            pl.BlockSpec((1, block_items, features), lambda i, plan: (plan[OWNER, i], 0, 0)),
            pl.BlockSpec((col_blocks, features, block_items), lambda i, plan: (0, 0, 0)),
        ),
        scratch_shapes=[
            pltpu.VMEM((block_items, features), jnp.float32),
            pltpu.VMEM((col_blocks, features, block_items), jnp.float32),
            pltpu.VMEM((block_items, block_items), jnp.bfloat16),
        ],
    )
    return pl.pallas_call(
        slots_kernel,
        out_shape=(
            jax.ShapeDtypeStruct((owners, block_items, features), jnp.int16),
            jax.ShapeDtypeStruct((col_blocks, features, block_items), jnp.int16),
        ),
        grid_spec=grid_spec,
        compiler_params=pltpu.CompilerParams(dimension_semantics=("arbitrary",)),
        name="slot_terms",
    )(plan, counts, row_pool, col_pool)


def exchange_kernel(row_terms, col_terms, row_in, col_in, stage, relay_one, relay_two, relay_y, send_sems, recv_sems, local_sems):
    x, z, y, core = place()
    half = row_terms.shape[2] // 2
    ring = [device(turn(x, d), y, z, core) for d in (1, -1)] + [device(x, y, turn(z, d), core) for d in (1, -1)]
    near_y = [device(x, turn(y, d), z, k) for d in (1, -1) for k in (0, 1)]
    partner = device(x, y, z, 1 - core)
    greet(ring + near_y + [partner])
    net = Copies(send_sems, recv_sems)
    here = ((x, z), (z, x))
    low, high = pl.ds(0, 2), pl.ds(2, 2)

    def rows_of(ref, way, first, second):
        piece = pl.ds(way * half, half)
        if way == 0:
            return ref.at[first, second, piece]
        return ref.at[second, first, piece]

    def to(way, stage_number, by):
        axis = way if stage_number == 0 else 1 - way
        if axis == 0:
            return device(turn(x, by), y, z, core)
        return device(x, y, turn(z, by), core)

    whole = pl.ds(0, SIDE)
    relayed, direct, passed, second, second_relay, second_pass, local = {}, {}, {}, {}, {}, {}, []
    for way in (0, 1):
        p, q = here[way]
        for by, pick in ((1, low), (-1, high)):
            relayed[way, by] = net.start(
                rows_of(row_terms, way, turn(p, 2), pick),
                relay_one.at[way, 0 if by == 1 else 1],
                to(way, 0, by),
            )
    y_relay = {}
    for at, by in enumerate((1, -1)):
        y_relay[by] = net.start(col_terms.at[turn(y, 2), whole_core(), at], relay_y.at[at], device(x, turn(y, by), z, core))
    for way in (0, 1):
        p, q = here[way]
        for by in (1, -1):
            direct[way, by] = net.start(
                rows_of(row_terms, way, turn(p, by), whole), stage.at[way, p], to(way, 0, by)
            )
    y_direct = []
    for by in (1, -1):
        for flip in (0, 1):
            k = lax.rem(core + flip, 2)
            y_direct.append(
                net.start(col_terms.at[turn(y, by), k], col_in.at[y, core], device(x, turn(y, by), z, k))
            )
    y_direct.append(net.start(col_terms.at[y, 1 - core], col_in.at[y, core], partner))

    def second_axis(way, origin, source):
        p, q = here[way]
        place_first = turn(p, origin)
        by_far = 1 if origin in (0, -1) else -1
        key = (way, origin)
        second_relay[key] = net.start(source(turn(q, 2)), relay_two.at[way, place_first], to(way, 1, by_far))
        for by in (1, -1):
            second[key + (by,)] = net.start(
                source(turn(q, by)), rows_of(row_in, way, place_first, q), to(way, 1, by)
            )
        if origin != 0:
            copy = pltpu.make_async_copy(source(q), rows_of(row_in, way, place_first, q), local_sems.at[len(local)])
            copy.start()
            local.append(copy)

    for way in (0, 1):
        p, q = here[way]
        second_axis(way, 0, lambda at, way=way, p=p: rows_of(row_terms, way, p, at))
    for way in (0, 1):
        p, q = here[way]
        for by, pick in ((1, low), (-1, high)):
            relayed[way, by].wait_recv()
            passed[way, by] = net.start(
                relay_one.at[way, 0 if by == 1 else 1], stage.at[way, turn(p, -by), pick], to(way, 0, by)
            )
    y_pass = []
    for at, by in enumerate((1, -1)):
        y_relay[by].wait_recv()
        for flip in (0, 1):
            k = lax.rem(core + flip, 2)
            y_pass.append(
                net.start(relay_y.at[at, k], col_in.at[turn(y, -by), core, at], device(x, turn(y, by), z, k))
            )

    def pass_on(origin):
        for way in (0, 1):
            p, q = here[way]
            by = 1 if origin in (0, -1) else -1
            second_relay[way, origin].wait_recv()
            place_first = turn(p, origin)
            second_pass[way, origin] = net.start(
                relay_two.at[way, place_first], rows_of(row_in, way, place_first, turn(q, -by)), to(way, 1, by)
            )

    for by in (1, -1):
        for way in (0, 1):
            p, q = here[way]
            direct[way, by].wait_recv()
            second_axis(way, -by, lambda at, way=way, p=p, by=by: stage.at[way, turn(p, -by), at])
    pass_on(0)
    for way in (0, 1):
        p, q = here[way]
        for by in (1, -1):
            passed[way, by].wait_recv()
        second_axis(way, 2, lambda at, way=way, p=p: stage.at[way, turn(p, 2), at])
    for origin in (-1, 1, 2):
        pass_on(origin)
    for copy in list(second.values()) + list(second_pass.values()) + y_direct + y_pass:
        copy.wait_recv()
    net.finish()
    for copy in local:
        copy.wait()


def whole_core():
    return pl.ds(0, 2)


EXCHANGE_COPIES = 2 * 22 + 2 + 5 + 4


def exchange(row_terms, col_terms):
    block_items, features = row_terms.shape[2:]
    half = block_items // 2
    return pl.pallas_call(
        exchange_kernel,
        out_shape=(
            jax.ShapeDtypeStruct(row_terms.shape, jnp.int16),
            jax.ShapeDtypeStruct(col_terms.shape, jnp.int16),
        ),
        in_specs=[ANY] * 2,
        out_specs=(ANY,) * 2,
        scratch_shapes=[
            pltpu.VMEM((2, SIDE, SIDE, half, features), jnp.int16),
            pltpu.VMEM((2, 2, 2, half, features), jnp.int16),
            pltpu.VMEM((2, SIDE, half, features), jnp.int16),
            pltpu.VMEM((2, 2) + col_terms.shape[3:], jnp.int16),
            pltpu.SemaphoreType.DMA((EXCHANGE_COPIES,)),
            pltpu.SemaphoreType.DMA((EXCHANGE_COPIES,)),
            pltpu.SemaphoreType.DMA((6,)),
        ],
        compiler_params=pltpu.CompilerParams(collective_id=1, has_side_effects=True),
        name="exchange_terms",
    )(row_terms, col_terms)


def update_kernel(
    where, sel_ref, row_in, row_own, col_in, col_own, row_embed, row_accum, col_embed, col_accum,
    row_out, col_out, row_sum, col_sum,
):
    row, col = where[0], where[1]
    row_sum[...] = jnp.zeros_like(row_sum)

    def add(source, code, block):
        @pl.when(block < row_sum.shape[0])
        def _():
            row_sum[block] += decode(code)

    def one(source, carry):
        @pl.when(source != row)
        def _():
            add(source, row_in[source], sel_ref[source, 0, 0])

        return carry

    lax.fori_loop(0, row_in.shape[0], one, 0)
    add(row, row_own[0], where[2])
    col_sum[...] = decode(col_own[0])

    def other(source, carry):
        @pl.when(source != col)
        def _():
            col_sum[...] += decode(col_in[source])

        return carry

    lax.fori_loop(0, col_in.shape[0], other, 0)

    def step(embed, accum, grad, out, block):
        total = accum[block] + grad * grad
        out[block] = embed[block] - (learning_rate * grad) * lax.rsqrt(total)

    for block in range(row_sum.shape[0]):
        step(row_embed, row_accum, row_sum[block], row_out, block)
        step(col_embed, col_accum, col_sum[block].T, col_out, block)


def update(where, sel_in, row_in, row_terms, col_in, col_terms, row_embed, row_accum, col_embed, col_accum):
    blocks, block_items, features = row_embed.shape
    owners, around = row_in.shape[0], col_in.shape[0]
    group = min(128, block_items)
    state = pl.BlockSpec((blocks, group, features), lambda i, where: (0, i, 0))
    shape = jax.ShapeDtypeStruct(row_embed.shape, jnp.float32)
    grid_spec = pltpu.PrefetchScalarGridSpec(
        num_scalar_prefetch=1,
        grid=(block_items // group,),
        in_specs=[
            pl.BlockSpec(memory_space=pltpu.SMEM),
            pl.BlockSpec((owners, group, features), lambda i, where: (0, i, 0)),
            pl.BlockSpec((1, group, features), lambda i, where: (where[0], i, 0)),
            pl.BlockSpec((around, blocks, features, group), lambda i, where: (0, 0, 0, i)),
            pl.BlockSpec((1, blocks, features, group), lambda i, where: (where[1], 0, 0, i)),
        ]
        + [state] * 4,
        out_specs=(state, state),
        scratch_shapes=[
            pltpu.VMEM((blocks, group, features), jnp.float32),
            pltpu.VMEM((blocks, features, group), jnp.float32),
        ],
    )
    return pl.pallas_call(
        update_kernel,
        out_shape=(shape, shape),
        grid_spec=grid_spec,
        compiler_params=pltpu.CompilerParams(dimension_semantics=("arbitrary",)),
        name="adagrad",
    )(where, sel_in, row_in, row_terms, col_in, col_terms, row_embed, row_accum, col_embed, col_accum)


def pack(embed, offset, block_items):
    features = embed.shape[1]
    blocks = embed.shape[0] // block_items
    half = embed.astype(jnp.bfloat16).reshape(blocks, block_items, features)
    shift = offset.reshape(blocks, block_items // features, features)
    shift = jnp.pad(shift, ((0, 0), (0, PAD - block_items // features), (0, 0)))
    return jnp.concatenate([half, shift], axis=1)


def make_plan(shard_rows, shard_cols, live, row_blocks, col_blocks):
    around, owners = SIDE * 2, SIDE * SIDE
    slots_count = shard_rows.shape[0]
    at = jnp.arange(slots_count, dtype=jnp.int32)
    listed = at < live
    owner = shard_rows // row_blocks // around
    block = shard_rows % row_blocks
    row = owner * row_blocks + block
    col = shard_cols // col_blocks % around * col_blocks + shard_cols % col_blocks
    key = jnp.where(listed, owner, owners) * slots_count + at
    rank = jnp.sum((key[None, :] < key[:, None]).astype(jnp.int32), axis=1)
    takes = (rank[None, :] == jnp.minimum(at, live - 1)[:, None]).astype(jnp.int32)
    ordered = jnp.sum(takes[None] * jnp.stack([at, owner, row, col])[:, None, :], axis=2)
    slot, owner_at, row_at, col_at = ordered
    real = listed
    row_first = jnp.where((at == 0) | (owner_at != jnp.roll(owner_at, 1)) | (at >= live), 1, 0)
    earlier = (col_at[None, :] == col_at[:, None]) & (at[None, :] < at[:, None])
    col_first = 1 - jnp.any(earlier, axis=1).astype(jnp.int32)
    ids = jnp.arange(around * col_blocks, dtype=jnp.int32)
    col_used = jnp.any((ids[:, None] == col[None, :]) & listed[None, :], axis=1).astype(jnp.int32)
    rows = [jnp.full((slots_count,), live, jnp.int32), slot, owner_at, row_at, col_at, row_first, col_first]
    plan = jnp.stack(rows)
    plan = jnp.pad(plan, ((0, 0), (0, 1)), constant_values=1)
    plan = jnp.concatenate([plan, jnp.pad(col_used, (0, slots_count + 1 - col_used.shape[0]))[None]], axis=0)
    ids = jnp.arange(owners, dtype=jnp.int32)
    mine = (owner[None, :] == ids[:, None]) & listed[None, :]
    chosen = jnp.min(jnp.where(mine, block[None, :], row_blocks), axis=1)
    return plan, chosen


def on_device(
    counts, shard_rows, shard_cols, listed, row_embed, row_accum, row_offset, col_embed, col_accum, col_offset
):
    block_items = counts.shape[1]
    features = row_embed.shape[1]
    row_blocks = row_embed.shape[0] // block_items
    col_blocks = col_embed.shape[0] // block_items
    row, col = lax.axis_index("rows"), lax.axis_index("cols")
    plan, chosen = make_plan(shard_rows, shard_cols, listed[0], row_blocks, col_blocks)
    row_packed = pack(row_embed, row_offset, block_items)
    col_packed = pack(col_embed, col_offset, block_items)
    tiles = jnp.broadcast_to(chosen[:, None, None], (SIDE * SIDE, 8, 128))
    row_pool, col_pool, sel_in = gather(row_packed, col_packed, tiles)
    row_terms, col_terms = slots(plan, counts, row_pool, col_pool)
    row_in, col_in = exchange(
        row_terms.reshape(SIDE, SIDE, block_items, features),
        col_terms.reshape(SIDE, 2, col_blocks, features, block_items),
    )
    where = jnp.stack([row, col, jnp.sum(jnp.where(jnp.arange(SIDE * SIDE) == row, chosen, 0))]).astype(jnp.int32)
    row_state = (row_blocks, block_items, features)
    col_state = (col_blocks, block_items, features)
    row_new, col_new = update(
        where,
        sel_in,
        row_in.reshape(row_terms.shape),
        row_terms,
        col_in.reshape(SIDE * 2, col_blocks, features, block_items),
        col_terms.reshape(SIDE * 2, col_blocks, features, block_items),
        row_embed.reshape(row_state),
        row_accum.reshape(row_state),
        col_embed.reshape(col_state),
        col_accum.reshape(col_state),
    )
    return (row_new.reshape(row_embed.shape), col_new.reshape(col_embed.shape))


def solution(mesh):
    devices = ("rows", "cols")
    in_specs = (P(devices, None, None), P(devices), P(devices), P(devices)) + (
        P(devices, None),
        P(devices, None),
        P(devices),
    ) * 2
    out_specs = (P(devices, None), P(devices, None))
    return jax.shard_map(on_device, mesh=mesh, in_specs=in_specs, out_specs=out_specs, check_vma=False)
```

time: 413 us -> 167 us (0.40)
  waiting for transfers between devices: 236 us -> 0 us
  Pallas kernels: 0 us -> 153 us
  local copies, waits for them, and re-layouts: 43.6 us -> 2.69 us
  other arithmetic: 49.8 us -> 9.19 us
  blocking collectives: 34.7 us -> 0 us
  matrix products: 34.3 us -> 0 us
  between operations: 13.9 us -> 1.45 us
    reduce_scatter x2 -> x0, waiting for transfers between devices: 163 us -> none  [the longest x1 112 us: on_device(): lax.psum_scatter(row_part.reshape(-1, features), 'rows', scatter_dimensio...]
    pallas_call x0 -> x4, Pallas kernels: none -> 153 us  [the longest x1 66.2 us: exchange(): pl.pallas_call(exchange_kernel, out_shape=(jax.ShapeDtypeStruct(row_terms...]
    all_gather x2 -> x0, waiting for transfers between devices: 72.6 us -> none  [the longest x1 72.6 us: on_device(): row_pool = lax.all_gather(row_half, 'rows', axis=0, tiled=True)]
    scatter-add x8 -> x0, other arithmetic: 36.9 us -> none  [the longest x4 19.8 us: one_turn(): col_grad.at[col_slots].add(col_terms)]
    all_gather x2 -> x0, blocking collectives: 34.7 us -> none  [the longest x1 21.2 us: on_device(): row_shifts = lax.all_gather(row_offset, 'rows', axis=0, tiled=True)]
    dot_general x12 -> x0, matrix products: 34.3 us -> none  [the longest x4 22.2 us: one_turn(): jnp.einsum('sbd,sed->sbe', row_vectors, col_vectors, preferred_element_ty...]
    gather x16 -> x0, local copies, waits for them, and re-layouts: 31.7 us -> none  [the longest x4 16 us: one_turn(): row_vectors = jnp.take(row_pool, row_slots, axis=0)]
    broadcast_in_dim x2 -> x1, local copies, waits for them, and re-layouts: 11.8 us -> 0.7 us  [on_device(): tiles = jnp.broadcast_to(chosen[:, None, None], (SIDE * SIDE, 8, 128))]
  transfers between devices with their start and end apart: 4 -> 0, of which waited for: 3 -> 0; matrix products, arithmetic and copies ran while one was open for 1% -> 0% of each run, Pallas kernels for 0% -> 0%
where the time goes in v1:
time: 167 us; the launch traced here: 166 us
  Pallas kernels  153 us (92%)
  other arithmetic  9.19 us (6%)
  local copies, waits for them, and re-layouts  2.69 us (2%)
    pallas_call x1, Pallas kernels, exchange(): pl.pallas_call(exchange_kernel, out_shape=(jax.ShapeDtypeStruct(row_terms...  66.2 us
    pallas_call x1, Pallas kernels, gather(): pl.pallas_call(gather_kernel, out_shape=(jax.ShapeDtypeStruct((owners,) +...  53.9 us
    pallas_call x1, Pallas kernels, slots(): pl.pallas_call(slots_kernel, out_shape=(jax.ShapeDtypeStruct((owners, blo...  21.5 us
    pallas_call x1, Pallas kernels, update(): pl.pallas_call(update_kernel, out_shape=(shape, shape), grid_spec=grid_sp...  11 us

profile of v1, /device:TPU:1, one launch (start us, length us, event | category | flops | bytes accessed | tf_op | source)
XLA Modules:
  0.0 165.9 jit_solution(15999734673727847116)
XLA Ops:
  1.4 0.7 fusion.14
  2.1 0.7 fusion.9
  2.8 0.1 fusion.8
  2.9 0.7 iota_add_fusion
  3.6 0.7 add_bitcast_fusion
  4.2 0.2 convert_reduce_fusion
  4.4 0.7 fusion.10
  5.1 1.3 pad_add_fusion.2.where
  6.5 0.7 reshape.133
  7.2 0.7 reshape.135
  7.9 0.1 compare_convert_fusion
  7.9 0.1 multiply_reduce_fusion
  8.1 0.6 slice.13
  8.7 0.7 or_select_fusion
  9.4 0.2 fusion.6
  9.6 0.6 select_add_fusion.plan
  10.2 0.7 broadcast_in_dim.32.sel_ref
  10.9 1.3 convert_element_type.31
  12.2 0.1 convert_element_type.32
  12.3 1.1 fusion.2
  13.3 53.9 %gather_blocks.1 = (bf16[16,2,528,256]{3,2,1,0:T(8,128)(2,1)}, bf16[8,2,528,256]{3,2,1,0:T(8,128)(2,1)}, s32[16,8,128]{2,1,0:T(8,128)}) custom-call(bf16[2,528,256]{2,1,0:T(8,128)(2,1)} %get-tuple-element.28.row_ref, bf16[2,528,256]{2,1,0:T(8,128)(2,1)} %get-tuple-element.29.col_ref, s32[16,8,128]{2,1,0:T(8,128)} %broadcast_in_dim.32.sel_ref), custom_call_target="tpu_custom_call" | custom-call | tf_op jit(solution)/shard_map/gather_blocks/pallas_call | solution.py:176
  67.3 21.5 %slot_terms.1 = (s16[16,512,256]{2,1,0:T(8,128)(2,1)}, s16[16,256,512]{2,1,0:T(8,128)(2,1)}) custom-call(s32[8,17]{1,0:T(8,128)} %select_add_fusion.plan, s32[16,512,512]{2,1,0:T(8,128)} %counts_ref.1, bf16[32,528,256]{2,1,0:T(8,128)(2,1)} %bitcast.38, bf16[16,528,256]{2,1,0:T(8,128)(2,1)} %bitcast.39), custom_call_target="tpu_custom_call" | custom-call | tf_op jit(solution)/shard_map/slot_terms/pallas_call | solution.py:292
  88.8 66.2 %exchange_terms.1 = (s16[4,4,512,256]{3,2,1,0:T(8,128)(2,1)}, s16[4,2,2,256,512]{4,3,2,1,0:T(8,128)(2,1)}) custom-call(s16[4,4,512,256]{3,2,1,0:T(8,128)(2,1)} %bitcast.35, s16[4,2,2,256,512]{4,3,2,1,0:T(8,128)(2,1)} %bitcast.36), custom_call_target="tpu_custom_call" | custom-call | tf_op jit(solution)/shard_map/exchange_terms/pallas_call | solution.py:429
  154.9 11.0 %adagrad.1 = (f32[2,512,256]{2,1,0:T(8,128)}, f32[2,512,256]{2,1,0:T(8,128)}) custom-call(s32[3]{0:T(128)} %pad_add_fusion.2.where, s32[16,8,128]{2,1,0:T(8,128)} %get-tuple-element.11.sel_ref, s16[16,512,256]{2,1,0:T(8,128)(2,1)} %bitcast.42, s16[16,512,256]{2,1,0:T(8,128)(2,1)} %get-tuple-element.14.row_own, s16[8,2,256,512]{3,2,1,0:T(8,128)(2,1)} %bitcast.43, ...), custom_call_target="tpu_custom_call" | custom-call | tf_op jit(solution)/shard_map/adagrad/pallas_call | solution.py:515
  (11 shorter events, 0.1 us)
Async XLA Ops:
  0.6 11.6 %copy-start = (f32[1024,256]{1,0:T(8,128)S(1)}, f32[1024,256]{1,0:T(8,128)}, u32[]{:S(2)}) copy-start(f32[1024,256]{1,0:T(8,128)} %param.17) | copy-start | bytes 3145732

commit v2 on v1

v2 whole, which is shorter than its diff:
```python
import functools

import jax
import jax.numpy as jnp
from jax import lax
from jax.experimental import pallas as pl
from jax.experimental.pallas import tpu as pltpu
from jax.sharding import PartitionSpec as P

learning_rate = 0.5
conf_base = 0.1
conf_scale = 0.25
SIDE = 4
PAD = 16
FLOOR = 1.0 / 16.0
CODE = 32766.0 / 30.0
MESH = pl.DeviceIdType.MESH
ANY = pl.BlockSpec(memory_space=pl.ANY)


def encode(term):
    level = jnp.log2(1.0 + jnp.abs(term) * (1.0 / FLOOR)) * CODE + 0.5
    whole = level.astype(jnp.int32)
    return jnp.where(term < 0.0, -whole, whole).astype(jnp.int16)


def decode(code):
    level = code.astype(jnp.int32).astype(jnp.float32)
    size = jnp.exp2(jnp.abs(level) * (1.0 / CODE)) * FLOOR - FLOOR
    return jnp.where(level < 0.0, -size, size)


def place():
    row, col = lax.axis_index("rows"), lax.axis_index("cols")
    return row // SIDE, row % SIDE, col // 2, col % 2


def device(x, y, z, core):
    return (x * SIDE + z, y * 2 + core)


def turn(at, by):
    return lax.rem(at + (by + SIDE), SIDE)


class Copies:
    def __init__(self, send_sems, recv_sems):
        self.send_sems, self.recv_sems, self.started = send_sems, recv_sems, []

    def start(self, source, target, to):
        at = len(self.started)
        copy = pltpu.make_async_remote_copy(
            src_ref=source,
            dst_ref=target,
            send_sem=self.send_sems.at[at],
            recv_sem=self.recv_sems.at[at],
            device_id=to,
            device_id_type=MESH,
        )
        copy.start()
        self.started.append(copy)
        return copy

    def finish(self):
        for copy in self.started:
            copy.wait_send()


def greet(peers):
    barrier = pltpu.get_barrier_semaphore()
    for peer in peers:
        pl.semaphore_signal(barrier, inc=1, device_id=peer, device_id_type=MESH)
    pl.semaphore_wait(barrier, len(peers))


def gather_kernel(row_ref, col_ref, sel_ref, row_pool, col_pool, sel_in, send_sems, recv_sems, local_sems):
    x, z, y, core = place()
    row, col = lax.axis_index("rows"), lax.axis_index("cols")
    block_items = row_ref.shape[1] - PAD
    parts = (pl.ds(0, block_items // 2), pl.ds(block_items // 2, block_items // 2 + PAD))
    others = [(dx, dz) for dx in range(SIDE) for dz in range(SIDE) if (dx, dz) != (0, 0)]
    far = [device(turn(x, dx), y, turn(z, dz), core) for dx, dz in others]
    along_y = [device(x, turn(y, d), z, core) for d in (1, -1)]
    partner = device(x, y, z, 1 - core)
    greet(far + along_y + [partner])
    net = Copies(send_sems, recv_sems)

    own_row = pltpu.make_async_copy(row_ref, row_pool.at[row], local_sems.at[0])
    own_col = pltpu.make_async_copy(col_ref, col_pool.at[col], local_sems.at[1])
    own_sel = pltpu.make_async_copy(sel_ref, sel_in.at[row], local_sems.at[2])

    def hop(axis, by):
        if axis == 0:
            return device(turn(x, by), y, z, core)
        return device(x, y, turn(z, by), core)

    def pool(block, first, second, part=None):
        dx, dz = (first, second) if block == 0 else (second, first)
        ref = row_pool.at[turn(x, dx) * SIDE + turn(z, dz), block]
        return ref if part is None else ref.at[parts[part]]

    def own(block, part=None):
        ref = row_ref.at[block]
        return ref if part is None else ref.at[parts[part]]

    axes = ((0, 1), (1, 0))
    one, two, relay_one, relay_two = {}, {}, {}, {}
    for block in (0, 1):
        for by in (1, -1):
            one[block, by] = net.start(own(block), pool(block, 0, 0), hop(axes[block][0], by))
    y_own = [net.start(col_ref, col_pool.at[col], to) for to in along_y]
    core_own = net.start(col_ref, col_pool.at[col], partner)
    for block in (0, 1):
        for by in (1, -1):
            two[block, 0, by] = net.start(own(block), pool(block, 0, 0), hop(axes[block][1], by))
    own_row.start()
    own_col.start()
    own_sel.start()
    chosen = [
        net.start(sel_ref, sel_in.at[row], to) for to in far
    ]
    for by in (1, -1):
        for block in (0, 1):
            one[block, by].wait_recv()
            part = 0 if by == 1 else 1
            relay_one[block, by] = net.start(
                pool(block, -by, 0, part), pool(block, -by, 0, part), hop(axes[block][0], by)
            )
            for way in (1, -1):
                two[block, -by, way] = net.start(
                    pool(block, -by, 0), pool(block, -by, 0), hop(axes[block][1], way)
                )
    col_of = lambda d: turn(y, d) * 2 + core
    to_core, relay_y = [], []
    for at, by in enumerate((1, -1)):
        y_own[at].wait_recv()
        half = 0 if by == 1 else 1
        source = col_pool.at[col_of(-by), half]
        relay_y.append(net.start(source, source, along_y[at]))
        to_core.append(net.start(col_pool.at[col_of(-by)], col_pool.at[col_of(-by)], partner))

    def second_relays(first):
        for by in (1, -1):
            for block in (0, 1):
                two[block, first, by].wait_recv()
                part = 0 if by == 1 else 1
                relay_two[block, first, by] = net.start(
                    pool(block, first, -by, part), pool(block, first, -by, part), hop(axes[block][1], by)
                )

    second_relays(0)
    for block in (0, 1):
        for by in (1, -1):
            relay_one[block, by].wait_recv()
        for way in (1, -1):
            two[block, 2, way] = net.start(pool(block, 2, 0), pool(block, 2, 0), hop(axes[block][1], way))
    for copy in relay_y:
        copy.wait_recv()
    to_core.append(net.start(col_pool.at[col_of(2)], col_pool.at[col_of(2)], partner))
    for first in (-1, 1, 2):
        second_relays(first)
    for copy in relay_two.values():
        copy.wait_recv()
    for copy in [core_own] + to_core + chosen:
        copy.wait_recv()
    net.finish()
    own_row.wait()
    own_col.wait()
    own_sel.wait()


GATHER_COPIES = 40 + 2 + 1 + 2 + 3 + 15


def gather(row_packed, col_packed, sel):
    blocks, tall, features = row_packed.shape
    owners, around = SIDE * SIDE, SIDE * 2
    return pl.pallas_call(
        gather_kernel,
        out_shape=(
            jax.ShapeDtypeStruct((owners,) + row_packed.shape, jnp.bfloat16),
            jax.ShapeDtypeStruct((around,) + col_packed.shape, jnp.bfloat16),
            jax.ShapeDtypeStruct((owners,) + sel.shape, jnp.int32),
        ),
        in_specs=[ANY] * 3,
        out_specs=(ANY,) * 3,
        scratch_shapes=[
            pltpu.SemaphoreType.DMA((GATHER_COPIES,)),
            pltpu.SemaphoreType.DMA((GATHER_COPIES,)),
            pltpu.SemaphoreType.DMA((3,)),
        ],
        compiler_params=pltpu.CompilerParams(collective_id=0, has_side_effects=True),
        name="gather_blocks",
    )(row_packed, col_packed, sel)


LIVE, SLOT, OWNER, ROW, COL, ROW_FIRST, ROW_LAST, COL_FIRST, COL_USED = range(9)


def slots_kernel(plan, counts_ref, row_ref, col_ref, row_out, col_out, row_sum, col_sum, slope_ref):
    at = pl.program_id(0)
    block_items, features = row_sum.shape
    group = min(128, block_items)

    def offsets(ref):
        wide = ref[0, block_items:, :].astype(jnp.float32)
        pieces = [wide[i : i + 1] for i in range(block_items // features)]
        return pieces[0] if len(pieces) == 1 else jnp.concatenate(pieces, axis=1)

    @pl.when(at < plan[LIVE, 0])
    def _():
        col_vectors = col_ref[0, :block_items, :]
        row_shift = jnp.broadcast_to(offsets(row_ref), (8, block_items)).T[:, :1]
        col_shift = offsets(col_ref)
        for first in range(0, block_items, group):
            rows = slice(first, first + group)
            scores = lax.dot_general(
                row_ref[0, rows, :], col_vectors, (((1,), (1,)), ((), ())), preferred_element_type=jnp.float32
            )
            cells = counts_ref[0, rows, :].astype(jnp.float32)
            floored = jnp.maximum(cells, 1.0)
            gap = scores - row_shift[rows] - col_shift - jnp.log(floored)
            weight = conf_base + conf_scale * (floored * lax.rsqrt(floored))
            slope = jnp.where(cells > 0.0, weight * gap, 0.5 * jnp.tanh(0.5 * gap) + 0.5)
            slope_ref[rows, :] = slope.astype(jnp.bfloat16)
        slope = slope_ref[...]
        row_term = jnp.dot(slope, col_vectors, preferred_element_type=jnp.float32)

        @pl.when(plan[ROW_FIRST, at] == 1)
        def _():
            row_sum[...] = row_term

        @pl.when(plan[ROW_FIRST, at] == 0)
        def _():
            row_sum[...] += row_term

        @pl.when(plan[ROW_LAST, at] == 1)
        def _():
            row_out[0] = encode(row_sum[...])

        col_term = lax.dot_general(
            row_ref[0, :block_items, :], slope, (((0,), (0,)), ((), ())), preferred_element_type=jnp.float32
        )
        which = plan[COL, at]

        @pl.when(plan[COL_FIRST, at] == 1)
        def _():
            col_sum[which] = col_term

        @pl.when(plan[COL_FIRST, at] == 0)
        def _():
            col_sum[which] += col_term

    @pl.when(at == pl.num_programs(0) - 1)
    def _():
        def one(which, carry):
            @pl.when(plan[COL_USED, which] == 1)
            def _():
                col_out[which] = encode(col_sum[which])

            @pl.when(plan[COL_USED, which] == 0)
            def _():
                col_out[which] = jnp.zeros(col_out.shape[1:], jnp.int16)

            return carry

        lax.fori_loop(0, col_out.shape[0], one, 0)


def slots(plan, counts, row_pool, col_pool):
    count, block_items, unused = counts.shape
    owners, row_blocks, tall, features = row_pool.shape
    row_pool = row_pool.reshape(-1, tall, features)
    col_pool = col_pool.reshape(-1, tall, features)
    col_blocks = col_pool.shape[0]
    grid_spec = pltpu.PrefetchScalarGridSpec(
        num_scalar_prefetch=1,
        grid=(count,),
        in_specs=[
            pl.BlockSpec((1, block_items, block_items), lambda i, plan: (plan[SLOT, i], 0, 0)),
            pl.BlockSpec((1, tall, features), lambda i, plan: (plan[ROW, i], 0, 0)),
            pl.BlockSpec((1, tall, features), lambda i, plan: (plan[COL, i], 0, 0)),
        ],
        out_specs=(
            pl.BlockSpec((1, block_items, features), lambda i, plan: (plan[OWNER, i], 0, 0)),
            pl.BlockSpec((col_blocks, features, block_items), lambda i, plan: (0, 0, 0)),
        ),
        scratch_shapes=[
            pltpu.VMEM((block_items, features), jnp.float32),
            pltpu.VMEM((col_blocks, features, block_items), jnp.float32),
            pltpu.VMEM((block_items, block_items), jnp.bfloat16),
        ],
    )
    return pl.pallas_call(
        slots_kernel,
        out_shape=(
            jax.ShapeDtypeStruct((owners, block_items, features), jnp.int16),
            jax.ShapeDtypeStruct((col_blocks, features, block_items), jnp.int16),
        ),
        grid_spec=grid_spec,
        compiler_params=pltpu.CompilerParams(dimension_semantics=("arbitrary",)),
        name="slot_terms",
    )(plan, counts, row_pool, col_pool)


def reduce_kernel(
    row_terms, col_terms, sel_ref, row_embed, row_accum, col_embed, col_accum,
    row_out, col_out,
    stage, relay_one, row_sum, row_mid, relay_two, row_fin,
    col_own, col_part, col_sum, col_mid, relay_y, col_fin, state, fresh,
    send_sems, recv_sems, local_sems,
):
    x, z, y, core = place()
    half = row_terms.shape[2] // 2
    blocks, features, items = col_terms.shape[2:]
    ring = [device(turn(x, d), y, z, core) for d in (1, -1)] + [device(x, y, turn(z, d), core) for d in (1, -1)]
    along_y = [device(x, turn(y, d), z, core) for d in (1, -1)]
    partner = device(x, y, z, 1 - core)
    greet(ring + along_y + [partner])
    net = Copies(send_sems, recv_sems)
    here = ((x, z), (z, x))
    low, high, whole = pl.ds(0, 2), pl.ds(2, 2), pl.ds(0, SIDE)
    ways = ((1, low), (-1, high))

    def rows_of(way, first, second):
        piece = pl.ds(way * half, half)
        if way == 0:
            return row_terms.at[first, second, piece]
        return row_terms.at[second, first, piece]

    def to(way, stage_number, by):
        axis = way if stage_number == 0 else 1 - way
        if axis == 0:
            return device(turn(x, by), y, z, core)
        return device(x, y, turn(z, by), core)

    local = []

    def fetch(source, target):
        copy = pltpu.make_async_copy(source, target, local_sems.at[len(local)])
        copy.start()
        local.append(copy)
        return copy

    part, relayed, direct = {}, {}, {}
    for by in (2, 1, -1, 0):
        at = turn(y, by)
        part[by] = net.start(col_terms.at[at, 1 - core], col_part.at[at], partner)
    for way in (0, 1):
        p = here[way][0]
        for at, (by, pick) in enumerate(ways):
            relayed[way, by] = net.start(rows_of(way, turn(p, 2), pick), relay_one.at[way, at], to(way, 0, by))
    for way in (0, 1):
        p = here[way][0]
        for by in (1, -1):
            direct[way, by] = net.start(rows_of(way, turn(p, by), whole), stage.at[way, p], to(way, 0, by))
    own_cols = {by: fetch(col_terms.at[turn(y, by), core], col_own.at[turn(y, by)]) for by in (2, 1, -1, 0)}
    own_rows = [fetch(rows_of(way, here[way][0], whole), stage.at[way, here[way][0]]) for way in (0, 1)]
    loads = [fetch(ref, state.at[i]) for i, ref in enumerate((col_embed, col_accum, row_embed, row_accum))]

    tall = min(32, features)

    def over(count, size, body):
        @pl.loop(0, count)
        def _(i):
            body(pl.ds(pl.multiple_of(i * size, size), size))

    y_relay, y_direct = {}, {}
    for by in (2, 1, -1):
        at = turn(y, by)
        own_cols[by].wait()
        part[by].wait_recv()
        slot = (2, 1, -1).index(by)
        for block in range(blocks):
            def body(rows, block=block, at=at, slot=slot):
                both = decode(col_own[at, block, rows, :]) + decode(col_part[at, block, rows, :])
                col_mid[slot, block, rows, :] = encode(both)

            over(features // tall, tall, body)
        if by == 2:
            for i, way_y in enumerate((1, -1)):
                y_relay[way_y] = net.start(col_mid.at[slot, i], relay_y.at[i], along_y[i])
        else:
            y_direct[by] = net.start(col_mid.at[slot], col_fin.at[y], along_y[0 if by == 1 else 1])

    passed = {}
    for way in (0, 1):
        p = here[way][0]
        for at, (by, pick) in enumerate(ways):
            relayed[way, by].wait_recv()
            passed[way, by] = net.start(relay_one.at[way, at], stage.at[way, turn(p, -by), pick], to(way, 0, by))

    own_cols[0].wait()
    part[0].wait_recv()
    for block in range(blocks):
        def body(rows, block=block):
            col_sum[block, rows, :] = decode(col_own[y, block, rows, :]) + decode(col_part[y, block, rows, :])

        over(features // tall, tall, body)

    def gain(way, origin, second):
        p, q = here[way]
        first = turn(p, origin)
        holder = first * SIDE + q if way == 0 else q * SIDE + first
        owner = p * SIDE + second if way == 0 else second * SIDE + p
        chosen = sel_ref[holder, 0, owner]
        return [(chosen == block).astype(jnp.float32) for block in range(2)]

    step = min(32, half)

    def gather_sum(way, origin, dq, keep, finish):
        p, q = here[way]
        second = turn(q, dq)
        first = turn(p, origin)
        weights = gain(way, origin, second)

        def body(rows):
            term = decode(stage[way, first, second, rows, :])
            for block in range(2):
                value = term * weights[block]
                if keep:
                    value = value + row_sum[way, dq % SIDE, block, rows, :]
                if finish:
                    row_mid[way, dq % SIDE, block, rows, :] = encode(value)
                else:
                    row_sum[way, dq % SIDE, block, rows, :] = value

        over(half // step, step, body)

    for way in (0, 1):
        own_rows[way].wait()
        for dq in range(SIDE):
            gather_sum(way, 0, dq, False, False)
    y_pass = {}
    for i, by in enumerate((1, -1)):
        y_relay[by].wait_recv()
        y_pass[by] = net.start(relay_y.at[i], col_fin.at[turn(y, -by), i], along_y[i])
    for by in (1, -1):
        for way in (0, 1):
            direct[way, by].wait_recv()
            for dq in range(SIDE):
                gather_sum(way, -by, dq, True, False)
    row_relay, row_direct = {}, {}
    for way in (0, 1):
        q = here[way][1]
        for by in (1, -1):
            passed[way, by].wait_recv()
        for dq in (2, 1, 3):
            gather_sum(way, 2, dq, True, True)
            if dq == 2:
                for i, by in enumerate((1, -1)):
                    row_relay[way, by] = net.start(row_mid.at[way, 2, i], relay_two.at[way, i], to(way, 1, by))
            else:
                by = 1 if dq == 1 else -1
                row_direct[way, by] = net.start(row_mid.at[way, dq], row_fin.at[way, q], to(way, 1, by))
    for way in (0, 1):
        gather_sum(way, 2, 0, True, False)

    def add_cols(origin, block):
        at = turn(y, origin)

        def body(rows):
            col_sum[block, rows, :] += decode(col_fin[at, block, rows, :])

        over(features // tall, tall, body)

    for by in (1, -1):
        y_direct[by].wait_recv()
        for block in range(blocks):
            add_cols(-by, block)

    row_pass = {}
    for way in (0, 1):
        q = here[way][1]
        for i, by in enumerate((1, -1)):
            row_relay[way, by].wait_recv()
            row_pass[way, by] = net.start(relay_two.at[way, i], row_fin.at[way, turn(q, -by), i], to(way, 1, by))

    for i, by in enumerate((1, -1)):
        y_pass[by].wait_recv()
        add_cols(2, i)
    loads[0].wait()
    loads[1].wait()

    def renew(which, block, rows, grad):
        total = state[2 * which + 1, block, rows, :] + grad * grad
        fresh[which, block, rows, :] = state[2 * which, block, rows, :] - (learning_rate * grad) * lax.rsqrt(total)

    wide = min(128, items)
    for block in range(blocks):
        def body(rows, block=block):
            renew(0, block, rows, col_sum[block, :, rows].T)

        over(items // wide, wide, body)
    stores = [pltpu.make_async_copy(fresh.at[0], col_out, local_sems.at[len(local)])]
    stores[0].start()
    loads[2].wait()
    loads[3].wait()

    for by in (1, -1):
        for way in (0, 1):
            q = here[way][1]
            row_direct[way, by].wait_recv()
            at = turn(q, -by)
            for block in range(2):
                def body(rows, way=way, at=at, block=block):
                    row_sum[way, 0, block, rows, :] += decode(row_fin[way, at, block, rows, :])

                over(half // step, step, body)
    for way in (0, 1):
        q = here[way][1]
        for i, by in enumerate((1, -1)):
            row_pass[way, by].wait_recv()
            at = turn(q, 2)

            @pl.loop(0, half // step)
            def _(n, way=way, at=at, block=i):
                rows = pl.ds(pl.multiple_of(n * step, step), step)
                grad = row_sum[way, 0, block, rows, :] + decode(row_fin[way, at, block, rows, :])
                renew(1, block, pl.ds(pl.multiple_of(way * half + n * step, step), step), grad)

    stores.append(pltpu.make_async_copy(fresh.at[1], row_out, local_sems.at[len(local) + 1]))
    stores[1].start()
    net.finish()
    for copy in stores:
        copy.wait()


REDUCE_COPIES = 4 + 4 + 4 + 2 + 2 + 4 + 2 + 4 + 4 + 4


def reduce_terms(row_terms, col_terms, sel_in, row_embed, row_accum, col_embed, col_accum):
    block_items, features = row_terms.shape[2:]
    half = block_items // 2
    wire, f32 = jnp.int16, jnp.float32
    col_block = col_terms.shape[2:]
    state = row_embed.shape
    shape = jax.ShapeDtypeStruct(state, f32)
    return pl.pallas_call(
        reduce_kernel,
        out_shape=(shape, shape),
        in_specs=[ANY] * 2 + [pl.BlockSpec(memory_space=pltpu.SMEM)] + [ANY] * 4,
        out_specs=(ANY,) * 2,
        scratch_shapes=[
            pltpu.VMEM((2, SIDE, SIDE, half, features), wire),
            pltpu.VMEM((2, 2, 2, half, features), wire),
            pltpu.VMEM((2, SIDE, 2, half, features), f32),
            pltpu.VMEM((2, SIDE, 2, half, features), wire),
            pltpu.VMEM((2, 2, half, features), wire),
            pltpu.VMEM((2, SIDE, 2, half, features), wire),
            pltpu.VMEM((SIDE,) + col_block, wire),
            pltpu.VMEM((SIDE,) + col_block, wire),
            pltpu.VMEM(col_block, f32),
            pltpu.VMEM((3,) + col_block, wire),
            pltpu.VMEM((2,) + col_block[1:], wire),
            pltpu.VMEM((SIDE,) + col_block, wire),
            pltpu.VMEM((4,) + state, f32),
            pltpu.VMEM((2,) + state, f32),
            pltpu.SemaphoreType.DMA((REDUCE_COPIES,)),
            pltpu.SemaphoreType.DMA((REDUCE_COPIES,)),
            pltpu.SemaphoreType.DMA((12,)),
        ],
        compiler_params=pltpu.CompilerParams(collective_id=1, has_side_effects=True),
        name="reduce_terms",
    )(row_terms, col_terms, sel_in, row_embed, row_accum, col_embed, col_accum)


def prepare_kernel(
    rows_ref, cols_ref, listed_ref, row_embed, row_shift, col_embed, col_shift,
    row_packed, col_packed, plan_ref, sel_ref, *, row_blocks, col_blocks,
):
    count = rows_ref.shape[0]
    around, owners = SIDE * 2, SIDE * SIDE
    live = listed_ref[0]
    lane = lax.broadcasted_iota(jnp.int32, (count, 128), 1)
    line = lax.broadcasted_iota(jnp.int32, (count, 128), 0)
    zero = jnp.zeros((count, 128), jnp.int32)
    lists = {"owner": [zero, zero], "block": [zero, zero], "col": [zero, zero]}
    for i in range(count):
        r, c = rows_ref[i], cols_ref[i]
        values = {
            "owner": r // (row_blocks * around),
            "block": r % row_blocks,
            "col": c // col_blocks % around * col_blocks + c % col_blocks,
        }
        for name, (down, across) in lists.items():
            lists[name] = [jnp.where(line == i, values[name], down), jnp.where(lane == i, values[name], across)]
    owner, owner_l = lists["owner"]
    block, unused = lists["block"]
    col, col_l = lists["col"]
    listed, listed_l = line < live, lane < live
    key = jnp.where(listed, owner, owners) * count + line
    key_l = jnp.where(listed_l, owner_l, owners) * count + lane

    def tally(truth, axis):
        return jnp.sum(jnp.where(truth, 1.0, 0.0), axis=axis, keepdims=True)

    rank = tally((key_l < key) & (lane < count), 1).astype(jnp.int32)
    mine = (owner_l == owner) & listed_l
    row_first = tally(mine & (key_l < key), 1) == 0.0
    row_last = tally(mine & (key_l > key), 1) == 0.0
    col_first = tally((col_l == col) & listed_l & (key_l < key), 1) == 0.0
    takes = rank == jnp.minimum(lane, live - 1)

    def ordered(value):
        return jnp.sum(jnp.where(takes, value, 0).astype(jnp.float32), axis=0, keepdims=True).astype(jnp.int32)

    plan_ref[...] = jnp.zeros_like(plan_ref)
    plan_ref[LIVE : LIVE + 1, :] = jnp.full((1, 128), live, jnp.int32)
    plan_ref[SLOT : SLOT + 1, :] = ordered(line)
    plan_ref[OWNER : OWNER + 1, :] = ordered(owner)
    plan_ref[ROW : ROW + 1, :] = ordered(owner * row_blocks + block)
    plan_ref[COL : COL + 1, :] = ordered(col)
    plan_ref[ROW_FIRST : ROW_FIRST + 1, :] = ordered(jnp.where(row_first, 1, zero))
    plan_ref[ROW_LAST : ROW_LAST + 1, :] = ordered(jnp.where(row_last, 1, zero))
    plan_ref[COL_FIRST : COL_FIRST + 1, :] = ordered(jnp.where(col_first, 1, zero))
    plan_ref[COL_USED : COL_USED + 1, :] = jnp.where(tally((col == lane) & listed, 0) > 0.0, 1, 0)
    hit = (owner == lane) & listed
    chosen = jnp.min(jnp.where(hit, block, row_blocks).astype(jnp.float32), axis=0, keepdims=True)
    sel_ref[...] = jnp.broadcast_to(chosen, (8, 128)).astype(jnp.int32)

    for embed, shift, packed in ((row_embed, row_shift, row_packed), (col_embed, col_shift, col_packed)):
        blocks, tall, features = packed.shape
        items = tall - PAD
        for at in range(blocks):
            packed[at, :items, :] = embed[at * items : (at + 1) * items, :].astype(jnp.bfloat16)
            wide = jnp.zeros((PAD, features), jnp.float32)
            place_at = lax.broadcasted_iota(jnp.int32, (PAD, features), 0)
            for i in range(items // features):
                n = at * (items // features) + i
                wide = jnp.where(place_at == i, shift[n : n + 1, :].astype(jnp.float32), wide)
            packed[at, items:, :] = wide.astype(jnp.bfloat16)


def prepare(shard_rows, shard_cols, listed, row_embed, row_offset, col_embed, col_offset, block_items):
    features = row_embed.shape[1]
    row_blocks, col_blocks = row_embed.shape[0] // block_items, col_embed.shape[0] // block_items
    scalars, vectors = pl.BlockSpec(memory_space=pltpu.SMEM), pl.BlockSpec(memory_space=pltpu.VMEM)
    return pl.pallas_call(
        functools.partial(prepare_kernel, row_blocks=row_blocks, col_blocks=col_blocks),
        out_shape=(
            jax.ShapeDtypeStruct((row_blocks, block_items + PAD, features), jnp.bfloat16),
            jax.ShapeDtypeStruct((col_blocks, block_items + PAD, features), jnp.bfloat16),
            jax.ShapeDtypeStruct((16, 128), jnp.int32),
            jax.ShapeDtypeStruct((8, 128), jnp.int32),
        ),
        in_specs=[scalars] * 3 + [vectors] * 4,
        out_specs=(vectors,) * 4,
        name="prepare",
    )(
        shard_rows,
        shard_cols,
        listed,
        row_embed,
        row_offset.reshape(-1, features),
        col_embed,
        col_offset.reshape(-1, features),
    )


def on_device(
    counts, shard_rows, shard_cols, listed, row_embed, row_accum, row_offset, col_embed, col_accum, col_offset
):
    block_items = counts.shape[1]
    features = row_embed.shape[1]
    row_blocks = row_embed.shape[0] // block_items
    col_blocks = col_embed.shape[0] // block_items
    row_packed, col_packed, plan, sel = prepare(
        shard_rows, shard_cols, listed, row_embed, row_offset, col_embed, col_offset, block_items
    )
    row_pool, col_pool, sel_in = gather(row_packed, col_packed, sel)
    row_terms, col_terms = slots(plan, counts, row_pool, col_pool)
    row_state = (row_blocks, block_items, features)
    col_state = (col_blocks, block_items, features)
    row_new, col_new = reduce_terms(
        row_terms.reshape(SIDE, SIDE, block_items, features),
        col_terms.reshape(SIDE, 2, col_blocks, features, block_items),
        sel_in,
        row_embed.reshape(row_state),
        row_accum.reshape(row_state),
        col_embed.reshape(col_state),
        col_accum.reshape(col_state),
    )
    return (row_new.reshape(row_embed.shape), col_new.reshape(col_embed.shape))


def solution(mesh):
    devices = ("rows", "cols")
    in_specs = (P(devices, None, None), P(devices), P(devices), P(devices)) + (
        P(devices, None),
        P(devices, None),
        P(devices),
    ) * 2
    out_specs = (P(devices, None), P(devices, None))
    return jax.shard_map(on_device, mesh=mesh, in_specs=in_specs, out_specs=out_specs, check_vma=False)
```

time: 167 us -> 148 us (0.89)
  Pallas kernels: 153 us -> 139 us
  other arithmetic: 9.19 us -> 0 us
  local copies, waits for them, and re-layouts: 2.69 us -> 7.04 us
    pallas_call x2, Pallas kernels: 77.1 us -> 49.2 us  [the longest x1 46.4 us: reduce_terms(): pl.pallas_call(reduce_kernel, out_shape=(shape, shape), in_specs=[ANY] *...]
    pallas_call x1, Pallas kernels: 21.5 us -> 35.6 us  [slots(): pl.pallas_call(slots_kernel, out_shape=(jax.ShapeDtypeStruct((owners, blo...]
    unnamed x2, local copies, waits for them, and re-layouts: 0.01 us -> 4.52 us
    another operation x5 -> x0, other arithmetic: 2.7 us -> none  [the longest x3 1.35 us: make_plan(): jnp.stack([at, owner, row, col])[:, None, :]]
where the time goes in v2:
time: 148 us; the launch traced here: 147 us
  Pallas kernels  139 us (94%)
  local copies, waits for them, and re-layouts  7.04 us (5%)
    pallas_call x1, Pallas kernels, gather(): pl.pallas_call(gather_kernel, out_shape=(jax.ShapeDtypeStruct((owners,) +...  54 us
    pallas_call x1, Pallas kernels, reduce_terms(): pl.pallas_call(reduce_kernel, out_shape=(shape, shape), in_specs=[ANY] *...  46.4 us
    pallas_call x1, Pallas kernels, slots(): pl.pallas_call(slots_kernel, out_shape=(jax.ShapeDtypeStruct((owners, blo...  35.6 us
    unnamed x2, local copies, waits for them, and re-layouts  4.52 us

profile of v2, /device:TPU:1, one launch (start us, length us, event | category | flops | bytes accessed | tf_op | source)
XLA Modules:
  0.0 147.1 jit_solution(2577367229518876091)
XLA Ops:
  1.3 1.3 reshape.40.row_shift
  2.6 1.2 reshape.41.col_shift
  3.8 2.8 %prepare.1 = (bf16[2,528,256]{2,1,0:T(8,128)(2,1)}, bf16[2,528,256]{2,1,0:T(8,128)(2,1)}, s32[16,128]{1,0:T(8,128)}, s32[8,128]{1,0:T(8,128)}) custom-call(s32[16]{0:T(128)} %rows_ref.1, s32[16]{0:T(128)} %cols_ref.1, s32[1]{0:T(128)S(6)} %copy.14.listed_ref, f32[1024,256]{1,0:T(8,128)} %row_embed.1, bf16[4,256]{1,0:T(4,128)(2,1)} %reshape.40.row_shift, ...), custom_call_target="tpu_custom_call" | custom-call | tf_op jit(solution)/shard_map/prepare/pallas_call | solution.py:639
  6.6 54.0 %gather_blocks.1 = (bf16[16,2,528,256]{3,2,1,0:T(8,128)(2,1)}, bf16[8,2,528,256]{3,2,1,0:T(8,128)(2,1)}, s32[16,8,128]{2,1,0:T(8,128)}) custom-call(bf16[2,528,256]{2,1,0:T(8,128)(2,1)} %get-tuple-element.14.row_ref, bf16[2,528,256]{2,1,0:T(8,128)(2,1)} %get-tuple-element.15.col_ref, s32[8,128]{1,0:T(8,128)} %get-tuple-element.16.sel_ref), custom_call_target="tpu_custom_call" | custom-call | tf_op jit(solution)/shard_map/gather_blocks/pallas_call | solution.py:178
  60.6 35.6 %slot_terms.1 = (s16[16,512,256]{2,1,0:T(8,128)(2,1)}, s16[16,256,512]{2,1,0:T(8,128)(2,1)}) custom-call(s32[16,128]{1,0:T(8,128)} %get-tuple-element.13.plan, s32[16,512,512]{2,1,0:T(8,128)} %counts_ref.1, bf16[32,528,256]{2,1,0:T(8,128)(2,1)} %bitcast.10, bf16[16,528,256]{2,1,0:T(8,128)(2,1)} %bitcast.11), custom_call_target="tpu_custom_call" | custom-call | tf_op jit(solution)/shard_map/slot_terms/pallas_call | solution.py:294
  96.2 46.4 %reduce_terms.1 = (f32[2,512,256]{2,1,0:T(8,128)}, f32[2,512,256]{2,1,0:T(8,128)}) custom-call(s16[4,4,512,256]{3,2,1,0:T(8,128)(2,1)} %bitcast.12, s16[4,2,2,256,512]{4,3,2,1,0:T(8,128)(2,1)} %bitcast.13, s32[16,8,128]{2,1,0:T(8,128)} %get-tuple-element.21.sel_ref, f32[2,512,256]{2,1,0:T(8,128)} %bitcast.14, f32[2,512,256]{2,1,0:T(8,128)} %bitcast.16, ...), custom_call_target="tpu_custom_call" | custom-call | tf_op jit(solution)/shard_map/reduce_terms/pallas_call | solution.py:539
  142.6 2.3 %copy.15 = f32[1024,256]{1,0:T(8,128)} copy(f32[1024,256]{1,0:T(8,128)} %bitcast.19) | data formatting | bytes 2097152
  144.8 2.3 %copy.16 = f32[1024,256]{1,0:T(8,128)} copy(f32[1024,256]{1,0:T(8,128)} %bitcast.18) | data formatting | bytes 2097152
